TPU v7x, 32 devices: a whole 2x2x4 slice. The times are simulated.
32 devices in a mesh: lon: 2 (over x), lat: 16 (over z, y, core).
Axes of the slice: x: 2, y: 2, z: 4, core: 2. Of those that a mesh axis runs over, the one named last changes fastest.
Arguments:
- state: bfloat16 [1, 128, 256, 128], P(None, 'lat', 'lon'), may hold values from -6 to 6
- mix_weight: bfloat16 [128, 2, 128, 128], P('lat'), may hold values from -0.375 to 0.375
- skip_weight: bfloat16 [128, 128], replicated, may hold values from -0.5 to 0.5
Outputs:
- output: bfloat16 [1, 128, 256, 128], P(None, 'lat', 'lon')
All inputs are finite; a program needn't handle non-finite values.
Results may differ from a plain program's by a relative error of at most 0.008.
Values may be sent and summed in bfloat16 or wider, within the bound.
A program may use at most 64 MiB of HBM per device.

v0:
```python
import math
import jax
import jax.numpy as jnp
from jax import lax
from jax.sharding import PartitionSpec as P

rescale_limit = 1e18
log_rescale = 18.0 * math.log(10.0)


def lat_geometry(lat_count):
    positions = jnp.arange(lat_count, dtype=jnp.float32)
    colatitude = jnp.pi * (positions + 0.5) / lat_count
    return (jnp.cos(colatitude), jnp.sin(colatitude))


def fourier_tables(lon_count, mode_count):
    lon_index = jnp.arange(lon_count, dtype=jnp.int32)[:, None]
    mode_index = jnp.arange(mode_count, dtype=jnp.int32)[None, :]
    angles = (lon_index * mode_index % lon_count).astype(jnp.float32) * (2.0 * math.pi / lon_count)
    norming = 1.0 / math.sqrt(lon_count)
    paired = jnp.stack([jnp.cos(angles), -jnp.sin(angles)], axis=2) * norming
    weight = jnp.where(mode_index == 0, 1.0, 2.0)[:, :, None]
    forward = paired.reshape(lon_count, 2 * mode_count).astype(jnp.bfloat16)
    backward = (paired * weight).reshape(lon_count, 2 * mode_count).astype(jnp.bfloat16)
    return (forward, backward)


def legendre_tables(mode_ids, lat_count, degrees):
    cosine, sine_values = lat_geometry(lat_count)
    count = mode_ids.shape[0]
    layout = (1, lat_count // 128, 128)
    orders = mode_ids.astype(jnp.float32)[:, None]
    counter = jnp.arange(1, degrees + 1, dtype=jnp.float32)
    halves = 0.5 * jnp.log((2.0 * counter + 1.0) / (2.0 * counter))
    summed = jnp.sum(
        jnp.where(counter[None, :] <= orders, halves[None, :], jnp.float32(0.0)),
        axis=1,
        keepdims=True,
    )
    log_start = 0.5 * jnp.log(jnp.float32(0.5)) + summed + orders * jnp.log(sine_values)[None, :]
    log_start = log_start.reshape((count,) + layout[1:])
    orders = orders.reshape(count, 1, 1)
    cosine = cosine.reshape(layout)
    sine_values = sine_values.reshape(layout)
    analysis_scale = math.pi / math.sqrt(lat_count)
    synthesis_scale = 1.0 / math.sqrt(degrees)
    zeros = jnp.zeros((count,) + layout[1:], jnp.float32)

    def advance(carry, level_index):
        previous, earlier, exponent = carry
        level = level_index.astype(jnp.float32)
        ratio_a = jnp.sqrt(
            jnp.maximum(4.0 * level * level - 1.0, 0.0)
            / jnp.maximum(level * level - orders * orders, 1.0)
        )
        below = level - 1.0
        ratio_b = jnp.sqrt(
            jnp.maximum(below * below - orders * orders, 0.0)
            / jnp.maximum(4.0 * below * below - 1.0, 1.0)
        )
        raised = ratio_a * (cosine * previous - ratio_b * earlier)
        at_start = level == orders
        current = jnp.where(at_start, 1.0, jnp.where(level > orders, raised, 0.0))
        exponent = jnp.where(at_start, log_start, exponent)
        oversize = jnp.abs(current) > rescale_limit
        factor = jnp.where(oversize, 1.0 / rescale_limit, 1.0)
        earlier = previous * factor
        previous = current * factor
        exponent = exponent + jnp.where(oversize, log_rescale, 0.0)
        value = previous * jnp.exp(exponent)
        analysis_row = (value * analysis_scale * sine_values).astype(jnp.bfloat16)
        synthesis_row = (value * synthesis_scale).astype(jnp.bfloat16)
        return ((previous, earlier, exponent), (analysis_row, synthesis_row))

    levels = jnp.arange(degrees, dtype=jnp.int32)
    outputs = lax.scan(advance, (zeros, zeros, zeros), levels, unroll=32)[1]
    analysis = outputs[0].reshape(degrees, count, lat_count)
    synthesis = outputs[1].reshape(degrees, count, lat_count)
    return (analysis, synthesis)


def mixing_blocks(mix_weight):
    real_part = mix_weight[:, 0]
    imag_part = mix_weight[:, 1]
    upper = jnp.concatenate([real_part, imag_part], axis=2)
    lower = jnp.concatenate([-imag_part, real_part], axis=2)
    return jnp.concatenate([upper, lower], axis=1)


def shards(state, mix_weight, skip_weight):
    samples, lat_dev, lon_dev, channels = state.shape
    lon_groups = lax.axis_size("lon")
    lat_groups = lax.axis_size("lat")
    lon_count = lon_dev * lon_groups
    lat_count = lat_dev * lat_groups
    mode_count = lon_count // 2
    lon_modes = mode_count // lon_groups
    own_modes = lon_modes // lat_groups
    forward, backward = fourier_tables(lon_count, mode_count)
    first_mode = lax.axis_index("lon") * lon_modes + lax.axis_index("lat") * own_modes
    mode_ids = first_mode + jnp.arange(own_modes, dtype=jnp.int32)
    analysis, synthesis = legendre_tables(mode_ids, lat_count, mode_count)
    block_weight = mixing_blocks(mix_weight)
    received = lax.all_to_all(state, "lon", split_axis=1, concat_axis=2, tiled=True)
    items = received.shape[0]
    row_count = received.shape[1]
    spectra = jnp.einsum(
        "sjkc,kq->sjqc", received, forward, preferred_element_type=jnp.float32
    ).astype(jnp.bfloat16)
    spectra = spectra.reshape(items, row_count, lon_groups, 2 * lon_modes, channels)
    spectra = lax.all_to_all(spectra, "lon", split_axis=2, concat_axis=1, tiled=True)
    spectrum = spectra.reshape(items, lat_dev, 2 * lon_modes, channels)
    received = lax.all_to_all(spectrum, "lat", split_axis=2, concat_axis=1, tiled=True)
    items = received.shape[0]
    pieces = received.reshape(items, lat_count, own_modes, 2, channels)
    coeffs = jnp.einsum(
        "lij,sjirc->slirc", analysis, pieces, preferred_element_type=jnp.float32
    ).astype(jnp.bfloat16)
    coeffs = coeffs.reshape(items, mode_count, 2 * own_modes, channels)
    coefficients = lax.all_to_all(coeffs, "lat", split_axis=1, concat_axis=2, tiled=True)
    deg_dev = coefficients.shape[1]
    paired = coefficients.reshape(samples, deg_dev, lon_modes, 2 * channels)
    mixed = jnp.einsum(
        "slix,lxy->sliy", paired, block_weight, preferred_element_type=jnp.float32
    ).astype(jnp.bfloat16)
    mixed = mixed.reshape(samples, deg_dev, 2 * lon_modes, channels)
    received = lax.all_to_all(mixed, "lat", split_axis=2, concat_axis=1, tiled=True)
    items = received.shape[0]
    pieces = received.reshape(items, mode_count, own_modes, 2 * channels)
    gridded = jnp.einsum(
        "lij,sliy->sjiy", synthesis, pieces, preferred_element_type=jnp.float32
    ).astype(jnp.bfloat16)
    gridded = gridded.reshape(items, lat_count, 2 * own_modes, channels)
    grid_modes = lax.all_to_all(gridded, "lat", split_axis=1, concat_axis=2, tiled=True)
    grid_modes = grid_modes.reshape(samples, lat_dev, 1, 2 * lon_modes, channels)
    received = lax.all_to_all(grid_modes, "lon", split_axis=1, concat_axis=2, tiled=True)
    items = received.shape[0]
    row_count = received.shape[1]
    spectra = received.reshape(items, row_count, 2 * mode_count, channels)
    values = jnp.einsum(
        "sjqc,kq->sjkc", spectra, backward, preferred_element_type=jnp.float32
    ).astype(jnp.bfloat16)
    spectral = lax.all_to_all(values, "lon", split_axis=2, concat_axis=1, tiled=True)
    local_term = jnp.einsum("sjkc,cd->sjkd", state, skip_weight, preferred_element_type=jnp.float32)
    return jax.nn.gelu(spectral.astype(jnp.float32) + local_term).astype(jnp.bfloat16)


def solution(mesh):
    placed = (P(None, "lat", "lon", None), P("lat", None, None, None), P())
    return jax.shard_map(
        shards, mesh=mesh, in_specs=placed, out_specs=P(None, "lat", "lon", None), check_vma=False
    )
```

profile of v0, /device:TPU:0, one launch (start us, length us, event | category | flops | bytes accessed | tf_op | source)
XLA Modules:
  0.0 206.9 jit_solution(11996657977514319588)
XLA Ops:
  0.0 4.4 %all-to-all-start = ((bf16[1,8,128,128]{3,2,0,1:T(8,128)(2,1)}), bf16[1,8,128,128]{3,2,0,1:T(8,128)(2,1)S(1)}, u32[]{:S(2)}, u32[]{:S(2)}) async-start(bf16[1,8,128,128]{3,2,0,1:T(8,128)(2,1)} %bitcast.1187), calls=%async_computation | async-start | bytes 524288 | tf_op jit(solution)/shard_map/all_to_all | solution.py:105
  4.4 0.5 sine_negate_fusion
  5.0 0.1 copy.339
  5.2 0.2 select_reduce_fusion
  5.4 4.8 %all-to-all-done = bf16[1,8,128,128]{3,2,0,1:T(8,128)(2,1)S(1)} async-done(((bf16[1,8,128,128]{3,2,0,1:T(8,128)(2,1)}), bf16[1,8,128,128]{3,2,0,1:T(8,128)(2,1)S(1)}, u32[]{:S(2)}, u32[]{:S(2)}) %all-to-all-start) | async-done | bytes 262176 | tf_op jit(solution)/shard_map/all_to_all | solution.py:105
  10.3 0.2 convolution_convert_fusion.4
  10.5 0.7 copy.342
  11.2 3.4 %all-to-all-start.1 = ((bf16[1,4,2,128,128]{4,3,1,0,2:T(8,128)(2,1)}), bf16[1,4,2,128,128]{4,3,1,0,2:T(8,128)(2,1)S(1)}, u32[]{:S(2)}, u32[]{:S(2)}) async-start(bf16[1,4,2,128,128]{4,3,1,0,2:T(8,128)(2,1)} %copy.342), calls=%async_computation.1 | async-start | bytes 524288 | tf_op jit(solution)/shard_map/all_to_all | solution.py:112
  14.8 5.1 %all-to-all-done.1 = bf16[1,4,2,128,128]{4,3,1,0,2:T(8,128)(2,1)S(1)} async-done(((bf16[1,4,2,128,128]{4,3,1,0,2:T(8,128)(2,1)}), bf16[1,4,2,128,128]{4,3,1,0,2:T(8,128)(2,1)S(1)}, u32[]{:S(2)}, u32[]{:S(2)}) %all-to-all-start.1) | async-done | bytes 262176 | tf_op jit(solution)/shard_map/all_to_all | solution.py:112
  19.8 0.9 copy.343
  20.7 6.2 %all-to-all-start.2 = ((bf16[1,8,128,128]{3,1,0,2:T(8,128)(2,1)}), bf16[1,8,128,128]{3,1,0,2:T(8,128)(2,1)S(1)}, u32[]{:S(2)}, u32[]{:S(2)}) async-start(bf16[1,8,128,128]{3,1,0,2:T(8,128)(2,1)} %copy.343), calls=%async_computation.2 | async-start | bytes 524288 | tf_op jit(solution)/shard_map/all_to_all | solution.py:114
  26.9 115.9 %while.25 = (s32[]{:T(128)}, f32[4,1,128]{2,0,1:T(4,128)S(1)}, f32[4,1,128]{2,0,1:T(4,128)S(1)}, f32[4,1,128]{2,0,1:T(4,128)S(1)}, bf16[4,32,4,1,128]{4,2,1,3,0:...) while((s32[]{:T(128)}, f32[4,1,128]{2,0,1:T(4,128)S(1)}, ...), condition=%wide.region_2.3_spmd.clone.clone.clone.clone, body=%wide.region_1.2_spmd.clone.clone.clone.clone.sunk | while | flops 619265 | bytes 824448 | solution.py:77
  27.0 0.7 fusion.393
  36.9 0.7 fusion.392
  51.6 0.1 constant_dynamic-update-slice_fusion.133
  51.8 0.1 constant_dynamic-update-slice_fusion.135
  52.1 0.1 constant_dynamic-update-slice_fusion.139
  52.3 0.1 constant_dynamic-update-slice_fusion.141
  52.9 0.1 constant_dynamic-update-slice_fusion.147
  53.5 0.1 constant_dynamic-update-slice_fusion.153
  54.0 0.1 constant_dynamic-update-slice_fusion.159
  56.0 0.7 fusion.393
  65.9 0.7 fusion.392
  80.3 0.1 constant_dynamic-update-slice_fusion.131
  80.9 0.1 constant_dynamic-update-slice_fusion.137
  81.5 0.1 constant_dynamic-update-slice_fusion.143
  82.1 0.1 constant_dynamic-update-slice_fusion.149
  82.3 0.1 constant_dynamic-update-slice_fusion.151
  82.6 0.1 constant_dynamic-update-slice_fusion.155
  82.8 0.1 constant_dynamic-update-slice_fusion.157
  85.0 0.7 fusion.393
  94.9 0.7 fusion.392
  109.5 0.1 constant_dynamic-update-slice_fusion.133
  109.7 0.1 constant_dynamic-update-slice_fusion.135
  110.1 0.1 constant_dynamic-update-slice_fusion.139
  110.3 0.1 constant_dynamic-update-slice_fusion.141
  110.6 0.1 constant_dynamic-update-slice_fusion.145
  110.8 0.1 constant_dynamic-update-slice_fusion.147
  111.4 0.1 constant_dynamic-update-slice_fusion.153
  112.0 0.1 constant_dynamic-update-slice_fusion.159
  113.9 0.7 fusion.393
  123.8 0.7 fusion.392
  138.3 0.1 constant_dynamic-update-slice_fusion.131
  142.8 0.2 copy.345
  143.0 0.3 convolution_convert_fusion.3
  143.3 0.9 copy.348
  144.2 6.0 %all-to-all-start.3 = ((bf16[1,128,8,128]{3,2,0,1:T(8,128)(2,1)}), bf16[1,128,8,128]{3,2,0,1:T(8,128)(2,1)S(1)}, u32[]{:S(2)}, u32[]{:S(2)}) async-start(bf16[1,128,8,128]{3,2,0,1:T(8,128)(2,1)} %copy.348), calls=%async_computation.3 | async-start | bytes 524288 | tf_op jit(solution)/shard_map/all_to_all | solution.py:121
  150.3 9.9 %all-to-all-done.3 = bf16[1,128,8,128]{3,2,0,1:T(8,128)(2,1)S(1)} async-done(((bf16[1,128,8,128]{3,2,0,1:T(8,128)(2,1)}), bf16[1,128,8,128]{3,2,0,1:T(8,128)(2,1)S(1)}, u32[]{:S(2)}, u32[]{:S(2)}) %all-to-all-start.3) | async-done | bytes 262176 | tf_op jit(solution)/shard_map/all_to_all | solution.py:121
  160.4 0.3 fusion.298
  160.8 0.2 copy.350
  160.9 12.7 %all_to_all.114 = bf16[1,8,128,128]{3,1,0,2:T(8,128)(2,1)S(1)} all-to-all(bf16[1,8,128,128]{3,1,0,2:T(8,128)(2,1)S(1)} %copy.350), channel_id=1, replica_groups=mesh['lon'=2,'lat'=16] {'lat'}, dimensions={2} | all-to-all | bytes 524288 | tf_op jit(solution)/shard_map/all_to_all | solution.py:128
  173.7 0.2 reshape.2627
  173.9 0.3 convolution_convert_fusion.2
  174.2 0.2 copy.355
  174.4 12.7 %all_to_all.115 = bf16[1,128,8,128]{3,2,0,1:T(8,128)(2,1)S(1)} all-to-all(bf16[1,128,8,128]{3,2,0,1:T(8,128)(2,1)S(1)} %copy.355), channel_id=1, replica_groups=mesh['lon'=2,'lat'=16] {'lat'}, dimensions={1} | all-to-all | bytes 524288 | tf_op jit(solution)/shard_map/all_to_all | solution.py:135
  187.1 0.8 copy.379
  187.8 3.4 %all-to-all-start.6 = ((bf16[1,8,1,128,128]{4,3,2,0,1:T(8,128)(2,1)}), bf16[1,8,1,128,128]{4,3,2,0,1:T(8,128)(2,1)S(1)}, u32[]{:S(2)}, u32[]{:S(2)}) async-start(bf16[1,8,1,128,128]{4,3,2,0,1:T(8,128)(2,1)} %bitcast.715), calls=%async_computation.6 | async-start | bytes 524288 | tf_op jit(solution)/shard_map/all_to_all | solution.py:137
  191.3 0.1 copy.336
  191.5 5.3 %all-to-all-done.6 = bf16[1,8,1,128,128]{4,3,2,0,1:T(8,128)(2,1)S(1)} async-done(((bf16[1,8,1,128,128]{4,3,2,0,1:T(8,128)(2,1)}), bf16[1,8,1,128,128]{4,3,2,0,1:T(8,128)(2,1)S(1)}, u32[]{:S(2)}, u32[]{:S(2)}) %all-to-all-start.6) | async-done | bytes 262176 | tf_op jit(solution)/shard_map/all_to_all | solution.py:137
  196.8 0.3 fusion.297
  197.1 0.2 copy.360
  197.3 7.6 %all_to_all.116 = bf16[1,4,256,128]{3,1,0,2:T(4,128)(2,1)S(1)} all-to-all(bf16[1,4,256,128]{3,1,0,2:T(4,128)(2,1)S(1)} %copy.360), channel_id=1, replica_groups=mesh['lon'=2,'lat'=16] {'lon'}, dimensions={2} | all-to-all | bytes 524288 | tf_op jit(solution)/shard_map/all_to_all | solution.py:144
  204.9 0.9 copy-done.2
  205.8 1.1 fusion.314
  (796 shorter events, 24.5 us)
Async XLA Ops:
  0.0 204.9 %copy-start = (bf16[128,128]{1,0:T(8,128)(2,1)S(1)}, bf16[128,128]{1,0:T(8,128)(2,1)}, u32[]{:S(2)}) copy-start(bf16[128,128]{1,0:T(8,128)(2,1)} %param.7) | copy-start | bytes 98308
  0.0 10.2 %all-to-all-start = ((bf16[1,8,128,128]{3,2,0,1:T(8,128)(2,1)}), bf16[1,8,128,128]{3,2,0,1:T(8,128)(2,1)S(1)}, u32[]{:S(2)}, u32[]{:S(2)}) async-start(bf16[1,8,128,128]{3,2,0,1:T(8,128)(2,1)} %bitcast.1187), calls=%async_computation | async-start | bytes 524288 | tf_op jit(solution)/shard_map/all_to_all | solution.py:105
  11.2 8.6 %all-to-all-start.1 = ((bf16[1,4,2,128,128]{4,3,1,0,2:T(8,128)(2,1)}), bf16[1,4,2,128,128]{4,3,1,0,2:T(8,128)(2,1)S(1)}, u32[]{:S(2)}, u32[]{:S(2)}) async-start(bf16[1,4,2,128,128]{4,3,1,0,2:T(8,128)(2,1)} %copy.342), calls=%async_computation.1 | async-start | bytes 524288 | tf_op jit(solution)/shard_map/all_to_all | solution.py:112
  20.7 122.1 %all-to-all-start.2 = ((bf16[1,8,128,128]{3,1,0,2:T(8,128)(2,1)}), bf16[1,8,128,128]{3,1,0,2:T(8,128)(2,1)S(1)}, u32[]{:S(2)}, u32[]{:S(2)}) async-start(bf16[1,8,128,128]{3,1,0,2:T(8,128)(2,1)} %copy.343), calls=%async_computation.2 | async-start | bytes 524288 | tf_op jit(solution)/shard_map/all_to_all | solution.py:114
  143.3 6.9 %copy-start.1 = (bf16[8,2,128,128]{3,2,1,0:T(8,128)(2,1)S(1)}, bf16[8,2,128,128]{3,2,1,0:T(8,128)(2,1)}, u32[]{:S(2)}) copy-start(bf16[8,2,128,128]{3,2,1,0:T(8,128)(2,1)} %param.6) | copy-start | bytes 1572868
  144.2 16.0 %all-to-all-start.3 = ((bf16[1,128,8,128]{3,2,0,1:T(8,128)(2,1)}), bf16[1,128,8,128]{3,2,0,1:T(8,128)(2,1)S(1)}, u32[]{:S(2)}, u32[]{:S(2)}) async-start(bf16[1,128,8,128]{3,2,0,1:T(8,128)(2,1)} %copy.348), calls=%async_computation.3 | async-start | bytes 524288 | tf_op jit(solution)/shard_map/all_to_all | solution.py:121
  187.8 9.0 %all-to-all-start.6 = ((bf16[1,8,1,128,128]{4,3,2,0,1:T(8,128)(2,1)}), bf16[1,8,1,128,128]{4,3,2,0,1:T(8,128)(2,1)S(1)}, u32[]{:S(2)}, u32[]{:S(2)}) async-start(bf16[1,8,1,128,128]{4,3,2,0,1:T(8,128)(2,1)} %bitcast.715), calls=%async_computation.6 | async-start | bytes 524288 | tf_op jit(solution)/shard_map/all_to_all | solution.py:137
  204.9 1.0 copy-start.2
where the time goes:
time: 209 us; the launch traced here: 207 us
  loops' own time  84.2 us (40%)
  blocking collectives  32.9 us (16%)
  other arithmetic  26.6 us (13%)
  waiting for transfers between devices  25.1 us (12%)
  starting transfers between devices  23.4 us (11%)
  local copies, waits for them, and re-layouts  11.8 us (6%)
  matrix products  2.38 us (1%)
    another operation x1, loops' own time, legendre_tables(): outputs = lax.scan(advance, (zeros, zeros, zeros), levels, unroll=32)[1]  84.2 us
    while x248, other arithmetic  18 us
    all_to_all x1, blocking collectives, shards(): lax.all_to_all(mixed, 'lat', split_axis=2, concat_axis=1, tiled=True)  12.7 us
    all_to_all x1, blocking collectives, shards(): lax.all_to_all(gridded, 'lat', split_axis=1, concat_axis=2, tiled=True)  12.7 us
    all_to_all x1, waiting for transfers between devices, shards(): lax.all_to_all(coeffs, 'lat', split_axis=1, concat_axis=2, tiled=True)  9.91 us
    all_to_all x1, blocking collectives, shards(): lax.all_to_all(values, 'lon', split_axis=2, concat_axis=1, tiled=True)  7.56 us
    all_to_all x1, starting transfers between devices, shards(): lax.all_to_all(spectrum, 'lat', split_axis=2, concat_axis=1, tiled=True)  6.19 us
    all_to_all x1, starting transfers between devices, shards(): lax.all_to_all(coeffs, 'lat', split_axis=1, concat_axis=2, tiled=True)  6 us
  transfers between devices with their start and end apart: 5, of which 4 were waited for; matrix products, arithmetic and copies ran while one was open for 16% of the time, Pallas kernels for 0%

commit v1 on v0

--- a/solution.py
+++ b/solution.py
@@ -125,7 +125,10 @@
         "slix,lxy->sliy", paired, block_weight, preferred_element_type=jnp.float32
     ).astype(jnp.bfloat16)
     mixed = mixed.reshape(samples, deg_dev, 2 * lon_modes, channels)
-    received = lax.all_to_all(mixed, "lat", split_axis=2, concat_axis=1, tiled=True)
+    received = jnp.concatenate(
+        lax.all_to_all(jnp.stack(jnp.split(mixed, lax.axis_size("lat"), axis=2)), "lat", 0, 0),
+        axis=1,
+    )
     items = received.shape[0]
     pieces = received.reshape(items, mode_count, own_modes, 2 * channels)
     gridded = jnp.einsum(

time: 209 us -> 209 us (level)
  no operation moved by 1% of the time
where the time goes in v1:
time: 209 us; the launch traced here: 207 us
  loops' own time  84.2 us (40%)
  blocking collectives  32.9 us (16%)
  other arithmetic  26.6 us (13%)
  waiting for transfers between devices  25.1 us (12%)
  starting transfers between devices  23.4 us (11%)
  local copies, waits for them, and re-layouts  11.8 us (6%)
  matrix products  2.38 us (1%)
    another operation x1, loops' own time, legendre_tables(): outputs = lax.scan(advance, (zeros, zeros, zeros), levels, unroll=32)[1]  84.2 us
    while x248, other arithmetic  18 us
    all_to_all x1, blocking collectives, shards(): lax.all_to_all(gridded, 'lat', split_axis=1, concat_axis=2, tiled=True)  12.7 us
    all_to_all x1, blocking collectives, shards(): lax.all_to_all(jnp.stack(jnp.split(mixed, lax.axis_size('lat'), axis=2)),...  12.7 us
    all_to_all x1, waiting for transfers between devices, shards(): lax.all_to_all(coeffs, 'lat', split_axis=1, concat_axis=2, tiled=True)  9.91 us
    all_to_all x1, blocking collectives, shards(): lax.all_to_all(values, 'lon', split_axis=2, concat_axis=1, tiled=True)  7.56 us
    all_to_all x1, starting transfers between devices, shards(): lax.all_to_all(spectrum, 'lat', split_axis=2, concat_axis=1, tiled=True)  6.19 us
    all_to_all x1, starting transfers between devices, shards(): lax.all_to_all(coeffs, 'lat', split_axis=1, concat_axis=2, tiled=True)  6 us
  transfers between devices with their start and end apart: 5, of which 4 were waited for; matrix products, arithmetic and copies ran while one was open for 16% of the time, Pallas kernels for 0%

profile of v1, /device:TPU:0, one launch (start us, length us, event | category | flops | bytes accessed | tf_op | source)
XLA Modules:
  0.0 206.9 jit_solution(11381531959015944369)
XLA Ops:
  0.0 4.4 %all-to-all-start = ((bf16[1,8,128,128]{3,2,0,1:T(8,128)(2,1)}), bf16[1,8,128,128]{3,2,0,1:T(8,128)(2,1)S(1)}, u32[]{:S(2)}, u32[]{:S(2)}) async-start(bf16[1,8,128,128]{3,2,0,1:T(8,128)(2,1)} %bitcast.1245), calls=%async_computation | async-start | bytes 524288 | tf_op jit(solution)/shard_map/all_to_all | solution.py:105
  4.4 0.5 sine_negate_fusion
  5.0 0.1 copy.297
  5.2 0.2 select_reduce_fusion
  5.4 4.8 %all-to-all-done = bf16[1,8,128,128]{3,2,0,1:T(8,128)(2,1)S(1)} async-done(((bf16[1,8,128,128]{3,2,0,1:T(8,128)(2,1)}), bf16[1,8,128,128]{3,2,0,1:T(8,128)(2,1)S(1)}, u32[]{:S(2)}, u32[]{:S(2)}) %all-to-all-start) | async-done | bytes 262176 | tf_op jit(solution)/shard_map/all_to_all | solution.py:105
  10.3 0.2 convolution_convert_fusion.4
  10.5 0.7 copy.300
  11.2 3.4 %all-to-all-start.1 = ((bf16[1,4,2,128,128]{4,3,1,0,2:T(8,128)(2,1)}), bf16[1,4,2,128,128]{4,3,1,0,2:T(8,128)(2,1)S(1)}, u32[]{:S(2)}, u32[]{:S(2)}) async-start(bf16[1,4,2,128,128]{4,3,1,0,2:T(8,128)(2,1)} %copy.300), calls=%async_computation.1 | async-start | bytes 524288 | tf_op jit(solution)/shard_map/all_to_all | solution.py:112
  14.8 5.1 %all-to-all-done.1 = bf16[1,4,2,128,128]{4,3,1,0,2:T(8,128)(2,1)S(1)} async-done(((bf16[1,4,2,128,128]{4,3,1,0,2:T(8,128)(2,1)}), bf16[1,4,2,128,128]{4,3,1,0,2:T(8,128)(2,1)S(1)}, u32[]{:S(2)}, u32[]{:S(2)}) %all-to-all-start.1) | async-done | bytes 262176 | tf_op jit(solution)/shard_map/all_to_all | solution.py:112
  19.8 0.9 copy.301
  20.7 6.2 %all-to-all-start.2 = ((bf16[1,8,128,128]{3,1,0,2:T(8,128)(2,1)}), bf16[1,8,128,128]{3,1,0,2:T(8,128)(2,1)S(1)}, u32[]{:S(2)}, u32[]{:S(2)}) async-start(bf16[1,8,128,128]{3,1,0,2:T(8,128)(2,1)} %copy.301), calls=%async_computation.2 | async-start | bytes 524288 | tf_op jit(solution)/shard_map/all_to_all | solution.py:114
  26.9 115.9 %while.25 = (s32[]{:T(128)}, f32[4,1,128]{2,0,1:T(4,128)S(1)}, f32[4,1,128]{2,0,1:T(4,128)S(1)}, f32[4,1,128]{2,0,1:T(4,128)S(1)}, bf16[4,32,4,1,128]{4,2,1,3,0:...) while((s32[]{:T(128)}, f32[4,1,128]{2,0,1:T(4,128)S(1)}, ...), condition=%wide.region_2.3_spmd.clone.clone.clone.clone, body=%wide.region_1.2_spmd.clone.clone.clone.clone.sunk | while | flops 619265 | bytes 824448 | solution.py:77
  27.0 0.7 fusion.393
  36.9 0.7 fusion.392
  51.6 0.1 constant_dynamic-update-slice_fusion.149
  51.8 0.1 constant_dynamic-update-slice_fusion.151
  52.1 0.1 constant_dynamic-update-slice_fusion.155
  52.3 0.1 constant_dynamic-update-slice_fusion.157
  52.9 0.1 constant_dynamic-update-slice_fusion.163
  53.5 0.1 constant_dynamic-update-slice_fusion.169
  54.0 0.1 constant_dynamic-update-slice_fusion.175
  56.0 0.7 fusion.393
  65.9 0.7 fusion.392
  80.3 0.1 constant_dynamic-update-slice_fusion.147
  80.9 0.1 constant_dynamic-update-slice_fusion.153
  81.5 0.1 constant_dynamic-update-slice_fusion.159
  82.1 0.1 constant_dynamic-update-slice_fusion.165
  82.3 0.1 constant_dynamic-update-slice_fusion.167
  82.6 0.1 constant_dynamic-update-slice_fusion.171
  82.8 0.1 constant_dynamic-update-slice_fusion.173
  85.0 0.7 fusion.393
  94.9 0.7 fusion.392
  109.5 0.1 constant_dynamic-update-slice_fusion.149
  109.7 0.1 constant_dynamic-update-slice_fusion.151
  110.1 0.1 constant_dynamic-update-slice_fusion.155
  110.3 0.1 constant_dynamic-update-slice_fusion.157
  110.6 0.1 constant_dynamic-update-slice_fusion.161
  110.8 0.1 constant_dynamic-update-slice_fusion.163
  111.4 0.1 constant_dynamic-update-slice_fusion.169
  112.0 0.1 constant_dynamic-update-slice_fusion.175
  113.9 0.7 fusion.393
  123.8 0.7 fusion.392
  138.3 0.1 constant_dynamic-update-slice_fusion.147
  138.8 0.1 constant_dynamic-update-slice_fusion.153
  142.8 0.2 copy.303
  143.0 0.3 convolution_convert_fusion.3
  143.3 0.9 copy.306
  144.2 6.0 %all-to-all-start.3 = ((bf16[1,128,8,128]{3,2,0,1:T(8,128)(2,1)}), bf16[1,128,8,128]{3,2,0,1:T(8,128)(2,1)S(1)}, u32[]{:S(2)}, u32[]{:S(2)}) async-start(bf16[1,128,8,128]{3,2,0,1:T(8,128)(2,1)} %copy.306), calls=%async_computation.3 | async-start | bytes 524288 | tf_op jit(solution)/shard_map/all_to_all | solution.py:121
  150.3 9.9 %all-to-all-done.3 = bf16[1,128,8,128]{3,2,0,1:T(8,128)(2,1)S(1)} async-done(((bf16[1,128,8,128]{3,2,0,1:T(8,128)(2,1)}), bf16[1,128,8,128]{3,2,0,1:T(8,128)(2,1)S(1)}, u32[]{:S(2)}, u32[]{:S(2)}) %all-to-all-start.3) | async-done | bytes 262176 | tf_op jit(solution)/shard_map/all_to_all | solution.py:121
  160.4 0.3 fusion.298
  161.1 12.7 %all_to_all.104 = bf16[16,1,8,8,128]{4,3,2,1,0:T(8,128)(2,1)S(1)} all-to-all(bf16[16,1,8,8,128]{4,3,2,1,0:T(8,128)(2,1)S(1)} %constant_dynamic-update-slice_fusion.64), channel_id=1, replica_groups=mesh['lon'=2,'lat'=16] {'lat'}, dimensions={0} | all-to-all | bytes 524288 | tf_op jit(solution)/shard_map/all_to_all | solution.py:129
  173.8 0.2 reshape.2625
  173.9 0.3 convolution_convert_fusion.2
  174.2 0.2 copy.310
  174.4 12.7 %all_to_all.105 = bf16[1,128,8,128]{3,2,0,1:T(8,128)(2,1)S(1)} all-to-all(bf16[1,128,8,128]{3,2,0,1:T(8,128)(2,1)S(1)} %copy.310), channel_id=1, replica_groups=mesh['lon'=2,'lat'=16] {'lat'}, dimensions={1} | all-to-all | bytes 524288 | tf_op jit(solution)/shard_map/all_to_all | solution.py:138
  187.1 0.8 copy.333
  187.9 3.4 %all-to-all-start.6 = ((bf16[1,8,1,128,128]{4,3,2,0,1:T(8,128)(2,1)}), bf16[1,8,1,128,128]{4,3,2,0,1:T(8,128)(2,1)S(1)}, u32[]{:S(2)}, u32[]{:S(2)}) async-start(bf16[1,8,1,128,128]{4,3,2,0,1:T(8,128)(2,1)} %bitcast.775), calls=%async_computation.6 | async-start | bytes 524288 | tf_op jit(solution)/shard_map/all_to_all | solution.py:140
  191.3 0.1 copy.294
  191.5 5.3 %all-to-all-done.6 = bf16[1,8,1,128,128]{4,3,2,0,1:T(8,128)(2,1)S(1)} async-done(((bf16[1,8,1,128,128]{4,3,2,0,1:T(8,128)(2,1)}), bf16[1,8,1,128,128]{4,3,2,0,1:T(8,128)(2,1)S(1)}, u32[]{:S(2)}, u32[]{:S(2)}) %all-to-all-start.6) | async-done | bytes 262176 | tf_op jit(solution)/shard_map/all_to_all | solution.py:140
  196.8 0.3 fusion.297
  197.1 0.2 copy.315
  197.3 7.6 %all_to_all.106 = bf16[1,4,256,128]{3,1,0,2:T(4,128)(2,1)S(1)} all-to-all(bf16[1,4,256,128]{3,1,0,2:T(4,128)(2,1)S(1)} %copy.315), channel_id=1, replica_groups=mesh['lon'=2,'lat'=16] {'lon'}, dimensions={2} | all-to-all | bytes 524288 | tf_op jit(solution)/shard_map/all_to_all | solution.py:147
  204.9 0.9 copy-done.2
  205.8 1.1 fusion.314
  (809 shorter events, 24.6 us)
Async XLA Ops:
  0.0 204.9 %copy-start = (bf16[128,128]{1,0:T(8,128)(2,1)S(1)}, bf16[128,128]{1,0:T(8,128)(2,1)}, u32[]{:S(2)}) copy-start(bf16[128,128]{1,0:T(8,128)(2,1)} %param.7) | copy-start | bytes 98308
  0.0 10.2 %all-to-all-start = ((bf16[1,8,128,128]{3,2,0,1:T(8,128)(2,1)}), bf16[1,8,128,128]{3,2,0,1:T(8,128)(2,1)S(1)}, u32[]{:S(2)}, u32[]{:S(2)}) async-start(bf16[1,8,128,128]{3,2,0,1:T(8,128)(2,1)} %bitcast.1245), calls=%async_computation | async-start | bytes 524288 | tf_op jit(solution)/shard_map/all_to_all | solution.py:105
  11.2 8.6 %all-to-all-start.1 = ((bf16[1,4,2,128,128]{4,3,1,0,2:T(8,128)(2,1)}), bf16[1,4,2,128,128]{4,3,1,0,2:T(8,128)(2,1)S(1)}, u32[]{:S(2)}, u32[]{:S(2)}) async-start(bf16[1,4,2,128,128]{4,3,1,0,2:T(8,128)(2,1)} %copy.300), calls=%async_computation.1 | async-start | bytes 524288 | tf_op jit(solution)/shard_map/all_to_all | solution.py:112
  20.7 122.1 %all-to-all-start.2 = ((bf16[1,8,128,128]{3,1,0,2:T(8,128)(2,1)}), bf16[1,8,128,128]{3,1,0,2:T(8,128)(2,1)S(1)}, u32[]{:S(2)}, u32[]{:S(2)}) async-start(bf16[1,8,128,128]{3,1,0,2:T(8,128)(2,1)} %copy.301), calls=%async_computation.2 | async-start | bytes 524288 | tf_op jit(solution)/shard_map/all_to_all | solution.py:114
  143.3 6.9 %copy-start.1 = (bf16[8,2,128,128]{3,2,1,0:T(8,128)(2,1)S(1)}, bf16[8,2,128,128]{3,2,1,0:T(8,128)(2,1)}, u32[]{:S(2)}) copy-start(bf16[8,2,128,128]{3,2,1,0:T(8,128)(2,1)} %param.6) | copy-start | bytes 1572868
  144.2 16.0 %all-to-all-start.3 = ((bf16[1,128,8,128]{3,2,0,1:T(8,128)(2,1)}), bf16[1,128,8,128]{3,2,0,1:T(8,128)(2,1)S(1)}, u32[]{:S(2)}, u32[]{:S(2)}) async-start(bf16[1,128,8,128]{3,2,0,1:T(8,128)(2,1)} %copy.306), calls=%async_computation.3 | async-start | bytes 524288 | tf_op jit(solution)/shard_map/all_to_all | solution.py:121
  187.9 9.0 %all-to-all-start.6 = ((bf16[1,8,1,128,128]{4,3,2,0,1:T(8,128)(2,1)}), bf16[1,8,1,128,128]{4,3,2,0,1:T(8,128)(2,1)S(1)}, u32[]{:S(2)}, u32[]{:S(2)}) async-start(bf16[1,8,1,128,128]{4,3,2,0,1:T(8,128)(2,1)} %bitcast.775), calls=%async_computation.6 | async-start | bytes 524288 | tf_op jit(solution)/shard_map/all_to_all | solution.py:140
  204.9 1.0 copy-start.2
